TPU v7x, 256 devices: a whole 4x4x8 slice. The times are simulated.
256 devices in a mesh: dp: 16 (over x, y), tensor: 16 (over z, core).
Axes of the slice: x: 4, y: 4, z: 8, core: 2. Of those that a mesh axis runs over, the one named last changes fastest.
Arguments:
- tokens: bfloat16 [32768, 1280], P(('dp', 'tensor'))
- cotangent: bfloat16 [32768, 1280], P(('dp', 'tensor')), may hold values from -6 to 6
- gate_weights: float32 [32768, 2], P(('dp', 'tensor')), may hold values from 0.2 to 1
- routes: int32 [32768, 2], P(('dp', 'tensor')), may hold values from 0 to 31, as said below
- slot_index: int32 [32768, 2], P(('dp', 'tensor')), may hold values from -1 to 1, as said below
- qkv_weight: bfloat16 [1280, 16, 240], P(None, 'tensor'), may hold values from -0.15625 to 0.15625
- proj_weight: bfloat16 [16, 80, 1280], P('tensor'), may hold values from -1.25 to 1.25
- up_weight: bfloat16 [32, 1280, 5120], P('dp', None, 'tensor'), may hold values from -0.15625 to 0.15625
- down_weight: bfloat16 [32, 5120, 1280], P('dp', 'tensor'), may hold values from -0.078125 to 0.078125
Outputs:
- layer_out: bfloat16 [32768, 1280], P(('dp', 'tensor'))
- gate_grad: float32 [32768, 2], P(('dp', 'tensor'))
- grad_qkv: float32 [1280, 16, 240], P('dp', 'tensor')
- grad_proj: float32 [16, 80, 1280], P('tensor', None, 'dp')
- grad_up: bfloat16 [32, 1280, 5120], P('dp', None, 'tensor')
- grad_down: bfloat16 [32, 5120, 1280], P('dp', 'tensor')
Inputs may be any that keep to these rules, and one draw needn't show every extreme that they name: `routes`: the two experts of a row differ. `slot_index`: -1 marks a dropped pair; within the rows of one device (aligned blocks of 128 rows) and one expert, the kept pairs hold the slots 0, 1, 2, ... without gaps, each at most once.
All inputs are finite; a program needn't handle non-finite values.
Results may differ from a plain program's by a relative error of at most 0.035.
Values may be sent and summed in bfloat16 or wider, within the bound.
A program may use at most 128 MiB of HBM per device.

v0:
```python
from functools import partial
import math
import jax
import jax.numpy as jnp
from jax import lax
from jax.sharding import PartitionSpec as P

CAP = 2
epsilon = 1e-06
half_root = 1.0 / math.sqrt(2.0)
bell_scale = 1.0 / math.sqrt(2.0 * math.pi)


def norm_parts(row_block):
    widened = row_block.astype(jnp.float32)
    center = widened - jnp.mean(widened, axis=-1, keepdims=True)
    factor = lax.rsqrt(jnp.mean(center * center, axis=-1, keepdims=True) + epsilon)
    return (center * factor, factor)


def norm_back(normal_rows, factor, upstream):
    mean_up = jnp.mean(upstream, axis=-1, keepdims=True)
    mean_mix = jnp.mean(upstream * normal_rows, axis=-1, keepdims=True)
    return factor * (upstream - mean_up - normal_rows * mean_mix)


def gelu_value(pre_act):
    return 0.5 * pre_act * (1.0 + lax.erf(pre_act * half_root))


def gelu_slope(pre_act):
    return (
        0.5 * (1.0 + lax.erf(pre_act * half_root))
        + pre_act * jnp.exp(-0.5 * pre_act * pre_act) * bell_scale
    )


def block_shares(query_block, key_rows, score_scale):
    scores = (
        jnp.einsum("qk,tk->qt", query_block, key_rows, preferred_element_type=jnp.float32)
        * score_scale
    )
    raised = jnp.exp(scores)
    return raised / jnp.sum(raised, axis=-1, keepdims=True)


def attend_head(queries, key_rows, value_rows, block_rows, score_scale):
    block_count = queries.shape[0] // block_rows

    def attend_one_block(query_block):
        shares = block_shares(query_block, key_rows, score_scale)
        context = jnp.dot(
            shares.astype(jnp.bfloat16), value_rows, preferred_element_type=jnp.float32
        )
        return context.astype(jnp.bfloat16)

    outputs = lax.map(attend_one_block, queries.reshape(block_count, block_rows, queries.shape[1]))
    return outputs.reshape(queries.shape)


def head_backward(queries, key_rows, value_rows, grad_context, block_rows, score_scale):
    block_count = queries.shape[0] // block_rows

    def head_one_block(carry, pieces):
        grad_keys, grad_values = carry
        query_block, grad_block = pieces
        shares = block_shares(query_block, key_rows, score_scale)
        grad_shares = jnp.einsum(
            "qk,tk->qt", grad_block, value_rows, preferred_element_type=jnp.float32
        )
        grad_scores = (
            shares
            * (grad_shares - jnp.sum(shares * grad_shares, axis=-1, keepdims=True))
            * score_scale
        ).astype(jnp.bfloat16)
        grad_query = jnp.dot(grad_scores, key_rows, preferred_element_type=jnp.float32).astype(
            jnp.bfloat16
        )
        grad_keys = grad_keys + jnp.einsum(
            "qt,qk->tk", grad_scores, query_block, preferred_element_type=jnp.float32
        )
        grad_values = grad_values + jnp.einsum(
            "qt,qk->tk", shares.astype(jnp.bfloat16), grad_block, preferred_element_type=jnp.float32
        )
        return ((grad_keys, grad_values), grad_query)

    zeros_rows = jnp.zeros(key_rows.shape, jnp.float32)
    shaped = (
        queries.reshape(block_count, block_rows, queries.shape[1]),
        grad_context.reshape(block_count, block_rows, queries.shape[1]),
    )
    (grad_keys, grad_values), grad_queries = lax.scan(
        head_one_block, (zeros_rows, zeros_rows), shaped
    )
    return (
        grad_queries.reshape(queries.shape),
        grad_keys.astype(jnp.bfloat16),
        grad_values.astype(jnp.bfloat16),
    )


def return_slots(expert_partial):
    summed = lax.psum_scatter(
        expert_partial.astype(jnp.bfloat16), "tensor", scatter_dimension=0, tiled=True
    ).astype(jnp.float32)
    returned = lax.all_to_all(
        summed[0].astype(jnp.bfloat16), "dp", split_axis=0, concat_axis=0, tiled=True
    )
    return returned.reshape(
        returned.shape[0] * returned.shape[1] * returned.shape[2], returned.shape[3]
    )


def shards(
    tokens,
    cotangent,
    gate_weights,
    routes,
    slot_index,
    qkv_weight,
    proj_weight,
    up_weight,
    down_weight,
):
    rows_dev, model_width = tokens.shape
    head_size = qkv_weight.shape[2] // 3
    score_scale = head_size ** (-0.5)
    group_count = lax.axis_size("dp")
    local_experts = up_weight.shape[0]
    places = group_count * local_experts * CAP
    normal_in, factor_in = norm_parts(tokens)
    normed = normal_in.astype(jnp.bfloat16)
    full_norm = lax.all_gather(normed, "tensor", axis=0, tiled=True)
    seq_len = full_norm.shape[0]
    block_rows = min(512, seq_len)
    qkv_rows = jnp.einsum(
        "sd,dhc->hsc", full_norm, qkv_weight, preferred_element_type=jnp.float32
    ).astype(jnp.bfloat16)
    queries = qkv_rows[:, :, :head_size]
    key_rows = qkv_rows[:, :, head_size : 2 * head_size]
    value_rows = qkv_rows[:, :, 2 * head_size :]
    context = jax.vmap(partial(attend_head, block_rows=block_rows, score_scale=score_scale))(
        queries, key_rows, value_rows
    )
    attention = lax.psum_scatter(
        jnp.einsum("hsk,hkd->sd", context, proj_weight, preferred_element_type=jnp.float32).astype(
            jnp.bfloat16
        ),
        "tensor",
        scatter_dimension=0,
        tiled=True,
    ).astype(jnp.float32)
    mid = (tokens.astype(jnp.float32) + attention).astype(jnp.bfloat16)
    normal_mid, factor_mid = norm_parts(mid)
    mid_normed = normal_mid.astype(jnp.bfloat16)
    slot_code = jnp.where(slot_index >= 0, routes * CAP + slot_index, -1)
    positions = jnp.arange(places, dtype=jnp.int32)
    pick_both = (slot_code[None, :, :] == positions[:, None, None]).astype(jnp.bfloat16)
    pick_first = pick_both[:, :, 0]
    pick_second = pick_both[:, :, 1]
    dispatch_rows = pick_first + pick_second
    outgoing = jnp.dot(dispatch_rows, mid_normed, preferred_element_type=jnp.float32).astype(
        jnp.bfloat16
    )
    outgoing = outgoing.reshape(group_count, local_experts, CAP, model_width)
    landed = lax.all_to_all(outgoing, "dp", split_axis=0, concat_axis=0, tiled=True)
    arrived = lax.all_gather(landed[None], "tensor", axis=0, tiled=True)
    pre_act = jnp.einsum("tsecd,edf->tsecf", arrived, up_weight, preferred_element_type=jnp.float32)
    hidden = gelu_value(pre_act).astype(jnp.bfloat16)
    expert_partial = jnp.einsum(
        "tsecf,efd->tsecd", hidden, down_weight, preferred_element_type=jnp.float32
    )
    returned = return_slots(expert_partial)
    expert_first = jnp.einsum("pr,pd->rd", pick_first, returned, preferred_element_type=jnp.float32)
    expert_second = jnp.einsum(
        "pr,pd->rd", pick_second, returned, preferred_element_type=jnp.float32
    )
    mixed_rows = gate_weights[:, 0:1] * expert_first + gate_weights[:, 1:2] * expert_second
    layer_out = (mid.astype(jnp.float32) + mixed_rows).astype(jnp.bfloat16)
    upstream = cotangent.astype(jnp.float32)
    gate_grad = jnp.stack(
        [jnp.sum(upstream * expert_first, axis=-1), jnp.sum(upstream * expert_second, axis=-1)],
        axis=1,
    )
    grad_first = (gate_weights[:, 0:1] * upstream).astype(jnp.bfloat16)
    grad_second = (gate_weights[:, 1:2] * upstream).astype(jnp.bfloat16)
    grad_outgoing = jnp.dot(pick_first, grad_first, preferred_element_type=jnp.float32) + jnp.dot(
        pick_second, grad_second, preferred_element_type=jnp.float32
    )
    grad_outgoing = grad_outgoing.astype(jnp.bfloat16).reshape(
        group_count, local_experts, CAP, model_width
    )
    grad_landed = lax.all_to_all(grad_outgoing, "dp", split_axis=0, concat_axis=0, tiled=True)
    grad_arrived = lax.all_gather(grad_landed[None], "tensor", axis=0, tiled=True)
    grad_hidden = jnp.einsum(
        "tsecd,efd->tsecf", grad_arrived, down_weight, preferred_element_type=jnp.float32
    )
    grad_pre = (grad_hidden * gelu_slope(pre_act)).astype(jnp.bfloat16)
    grad_down = jnp.einsum(
        "tsecf,tsecd->efd", hidden, grad_arrived, preferred_element_type=jnp.float32
    ).astype(jnp.bfloat16)
    grad_up = jnp.einsum(
        "tsecd,tsecf->edf", arrived, grad_pre, preferred_element_type=jnp.float32
    ).astype(jnp.bfloat16)
    grad_partial = jnp.einsum(
        "tsecf,edf->tsecd", grad_pre, up_weight, preferred_element_type=jnp.float32
    )
    grad_back = return_slots(grad_partial)
    grad_norm = jnp.einsum(
        "pr,pd->rd", dispatch_rows, grad_back, preferred_element_type=jnp.float32
    )
    grad_mid = (upstream + norm_back(normal_mid, factor_mid, grad_norm)).astype(jnp.bfloat16)
    full_grad = lax.all_gather(grad_mid, "tensor", axis=0, tiled=True)
    grad_context = jnp.einsum(
        "sd,hkd->hsk", full_grad, proj_weight, preferred_element_type=jnp.float32
    ).astype(jnp.bfloat16)
    grad_proj = jnp.einsum("hsk,sd->hkd", context, full_grad, preferred_element_type=jnp.float32)
    grad_queries, grad_keys, grad_values = jax.vmap(
        partial(head_backward, block_rows=block_rows, score_scale=score_scale)
    )(queries, key_rows, value_rows, grad_context)
    grad_rows = jnp.concatenate([grad_queries, grad_keys, grad_values], axis=-1)
    grad_qkv = jnp.einsum("sd,hsc->dhc", full_norm, grad_rows, preferred_element_type=jnp.float32)
    grad_qkv, grad_proj = (
        lax.psum_scatter(
            grad_qkv.astype(jnp.bfloat16), "dp", scatter_dimension=0, tiled=True
        ).astype(jnp.float32),
        lax.psum_scatter(
            grad_proj.astype(jnp.bfloat16), "dp", scatter_dimension=2, tiled=True
        ).astype(jnp.float32),
    )
    return (layer_out, gate_grad, grad_qkv, grad_proj, grad_up, grad_down)


def solution(mesh):
    return jax.shard_map(
        shards,
        mesh=mesh,
        in_specs=(
            P(("dp", "tensor"), None),
            P(("dp", "tensor"), None),
            P(("dp", "tensor"), None),
            P(("dp", "tensor"), None),
            P(("dp", "tensor"), None),
            P(None, "tensor", None),
            P("tensor", None, None),
            P("dp", None, "tensor"),
            P("dp", "tensor", None),
        ),
        out_specs=(
            P(("dp", "tensor"), None),
            P(("dp", "tensor"), None),
            P("dp", "tensor", None),
            P("tensor", None, "dp"),
            P("dp", None, "tensor"),
            P("dp", "tensor", None),
        ),
        check_vma=False,
    )
```

profile of v0, /device:TPU:2, one launch (start us, length us, event | category | flops | bytes accessed | tf_op | source)
XLA Modules:
  0.0 631.2 jit_solution(2711527637385925915)
XLA Ops:
  9.7 1.9 fusion.87
  11.7 46.4 %all-gather.7.cloned.1.call-done = bf16[2048,1280]{1,0:T(8,128)(2,1)} async-done(((bf16[128,1280]{1,0:T(8,128)(2,1)}), bf16[2048,1280]{1,0:T(8,128)(2,1)}) %all-gather.7.cloned.1.call-update) | async-done | bytes 5242896 | tf_op jit(solution)/shard_map/all_gather | solution.py:133
  58.0 4.2 fusion.47
  63.9 8.0 %while.25 = (s32[]{:T(128)}, bf16[4,1,512,80]{2,3,1,0:T(8,128)(2,1)S(1)}, bf16[4,1,512,80]{3,2,1,0:T(8,128)(2,1)S(1)}, bf16[1,2048,80]{2,1,0:T(8,128)(2,1)S(1)}, bf16[1,2048,80]{2,1,0:T(8,128)(2,1)}, /*index=5*/s32[]{:T(128)}) while((s32[]{:T(128)}, bf16[4,1,512,80]{2,3,1,0:T(8,128)(2,1)S(1)}, bf16[4,1,512,80]{3,2,1,0:T(8,128)(2,1)S(1)}, ...), condition=%wide.region_4.5_spmd, body=%wide.region_2.4_spmd.sunk | while | flops 340827648 | bytes 10965105 | solution.py:57
  72.3 3.9 convolution_convert_fusion.1
  77.6 62.2 %reduce-scatter.12.cloned.1.call-done = bf16[128,1280]{1,0:T(8,128)(2,1)} async-done(((bf16[2048,1280]{1,0:T(8,128)(2,1)}), bf16[128,1280]{1,0:T(8,128)(2,1)}) %reduce-scatter.12.cloned.1.call-update) | async-done | bytes 327696 | tf_op jit(solution)/shard_map/reduce_scatter | solution.py:145
  141.7 1.7 convolution_convert_fusion.8
  145.1 13.8 %all_to_all.20 = bf16[16,2,2,1280]{3,2,1,0:T(2,128)(2,1)S(1)} all-to-all(bf16[16,2,2,1280]{3,2,1,0:T(2,128)(2,1)} %reshape.172), channel_id=1, replica_groups=mesh['dp'=16,'tensor'=16] {'dp'}, dimensions={0} | all-to-all | bytes 327680 | tf_op jit(solution)/shard_map/all_to_all | solution.py:166
  161.7 1.7 fusion.48
  165.0 11.6 %all_to_all.21 = bf16[16,2,2,1280]{3,2,1,0:T(2,128)(2,1)S(1)} all-to-all(bf16[16,2,2,1280]{3,2,1,0:T(2,128)(2,1)} %reshape.174), channel_id=1, replica_groups=mesh['dp'=16,'tensor'=16] {'dp'}, dimensions={0} | all-to-all | bytes 327680 | tf_op jit(solution)/shard_map/all_to_all | solution.py:193
  177.5 19.0 %all-gather.11.cloned.1.call-done = bf16[256,2,2,1280]{3,0,2,1:T(8,128)(2,1)} async-done(((bf16[16,2,2,1280]{3,0,2,1:T(8,128)(2,1)}), bf16[256,2,2,1280]{3,0,2,1:T(8,128)(2,1)}) %all-gather.11.cloned.1.call-update) | async-done | bytes 2621456 | tf_op jit(solution)/shard_map/all_gather | solution.py:167
  196.6 4.7 fusion.62
  201.2 36.6 %all-gather.13.cloned.1.call-done = bf16[256,2,2,1280]{3,0,2,1:T(8,128)(2,1)} async-done(((bf16[16,2,2,1280]{3,0,2,1:T(8,128)(2,1)}), bf16[256,2,2,1280]{3,0,2,1:T(8,128)(2,1)}) %all-gather.13.cloned.1.call-update) | async-done | bytes 2621456 | tf_op jit(solution)/shard_map/all_gather | solution.py:194
  237.8 4.3 fusion.60
  243.0 3.0 fusion.38
  246.0 3.0 fusion.37
  250.3 122.9 %all-reduce.9.cloned.1.call-done = (bf16[16,16,2,2,1280]{4,1,3,0,2:T(8,128)(2,1)}, bf16[16,16,2,2,1280]{4,1,3,0,2:T(8,128)(2,1)}) async-done(((bf16[16,16,2,2,1280]{4,1,3,0,2:T(8,128)(2,1)}, bf16[16,16,2,2,1280]{4,1,3,0,2:T(8,128)(2,1)}), (bf16[16,16,2,2,1280]{4,1,3,0,2:T(8,128)(2,1)}, bf16[16,16,2,2,1280]{4,1,3,0,2:T(8,128)(2,1)})) %all-reduce.9.cloned.1.call-update) | async-done | bytes 5242896
  375.5 7.3 %all-to-all-start.3 = ((bf16[16,2,2,1280]{3,2,1,0:T(2,128)(2,1)}), bf16[16,2,2,1280]{3,2,1,0:T(2,128)(2,1)S(1)}, u32[]{:S(2)}, u32[]{:S(2)}) async-start(bf16[16,2,2,1280]{3,2,1,0:T(2,128)(2,1)} %copy.57), calls=%async_computation.4 | async-start | bytes 327680 | tf_op jit(solution)/shard_map/all_to_all | solution.py:106
  385.2 4.1 all-to-all-done.3
  389.3 5.1 all-to-all-start.1
  394.6 1.9 fusion.114
  396.5 4.4 all-to-all-done.1
  401.3 3.0 fusion.90
  406.3 4.0 fusion.40
  410.2 35.1 %all-gather.9.cloned.1.call-done = bf16[2048,1280]{1,0:T(8,128)(2,1)} async-done(((bf16[128,1280]{1,0:T(8,128)(2,1)}), bf16[2048,1280]{1,0:T(8,128)(2,1)}) %all-gather.9.cloned.1.call-update) | async-done | bytes 5242896 | tf_op jit(solution)/shard_map/all_gather | solution.py:213
  445.3 4.2 fusion.50
  449.8 4.2 fusion.49
  455.1 23.7 %while.26 = (s32[]{:T(128)}, f32[1,2048,80]{1,2,0:T(8,128)S(1)}, f32[1,2048,80]{1,2,0:T(8,128)S(1)}, bf16[4,1,512,80]{2,3,1,0:T(8,128)(2,1)S(1)}, bf16[4,1,512,8...) while((s32[]{:T(128)}, f32[1,2048,80]{1,2,0:T(8,128)S(1)}, ...), condition=%wide.region_17.18_spmd.clone, body=%wide.region_14.17_spmd.clone.sunk | while | flops 855284736 | bytes 37580964 | solution.py:92
  478.9 4.0 convolution_convert_fusion.4
  484.0 4.1 fusion.39
  488.7 52.8 %all-reduce.7.cloned.1.call-done = bf16[1,80,1280]{2,1,0:T(8,128)(2,1)} async-done(((bf16[1,80,1280]{2,1,0:T(8,128)(2,1)}), bf16[1,80,1280]{2,1,0:T(8,128)(2,1)}) %all-reduce.7.cloned.1.call-update) | async-done | bytes 204816
  543.0 79.8 %reduce-scatter.14.cloned.1.call-done = bf16[80,240]{1,0:T(8,128)(2,1)} async-done(((bf16[1280,240]{1,0:T(8,128)(2,1)}), bf16[80,240]{1,0:T(8,128)(2,1)}) %reduce-scatter.14.cloned.1.call-update) | async-done | bytes 38416
  (158 shorter events, 61.0 us)
Async XLA Ops:
  7.2 189.4 %copy-start = (bf16[2,1280,320]{1,2,0:T(8,128)(2,1)S(1)}, bf16[2,1280,320]{1,2,0:T(8,128)(2,1)}, u32[]{:S(2)}) copy-start(bf16[2,1280,320]{1,2,0:T(8,128)(2,1)} %param.20) | copy-start | bytes 4915204
  7.2 50.8 %all-gather.7.cloned.1.call-start = ((), (), s32[]{:S(2)}) async-start(), calls=%async_computation.6 | async-start | bytes 5570560 | tf_op jit(solution)/shard_map/all_gather | solution.py:133
  11.6 128.1 %reduce-scatter.12.cloned.1.call-start = ((), (), s32[]{:S(2)}) async-start(), calls=%async_computation.7 | async-start | bytes 5570560 | tf_op jit(solution)/shard_map/reduce_scatter | solution.py:145
  63.9 8.4 %copy-start.7 = (bf16[1,80,1280]{2,1,0:T(8,128)(2,1)S(1)}, bf16[1,80,1280]{2,1,0:T(8,128)(2,1)}, u32[]{:S(2)}) copy-start(bf16[1,80,1280]{2,1,0:T(8,128)(2,1)} %param.19) | copy-start | bytes 614404
  63.9 1.1 copy-start.13
  76.2 63.5 %copy-start.2 = (bf16[128,1280]{1,0:T(8,128)(2,1)S(1)}, bf16[128,1280]{1,0:T(8,128)(2,1)}, u32[]{:S(2)}) copy-start(bf16[128,1280]{1,0:T(8,128)(2,1)} %param.13) | copy-start | bytes 983044
  76.3 120.3 %all-gather.11.cloned.1.call-start = ((), (), s32[]{:S(2)}) async-start(), calls=%async_computation.9 | async-start | bytes 2785280 | tf_op jit(solution)/shard_map/all_gather | solution.py:167
  140.9 20.8 %copy-start.6 = (bf16[128,1280]{1,0:T(8,128)(2,1)S(1)}, bf16[128,1280]{1,0:T(8,128)(2,1)}, u32[]{:S(2)}) copy-start(bf16[128,1280]{1,0:T(8,128)(2,1)} %param.14) | copy-start | bytes 983044
  159.5 78.3 %all-gather.13.cloned.1.call-start = ((), (), s32[]{:S(2)}) async-start(), calls=%async_computation.10 | async-start | bytes 2785280 | tf_op jit(solution)/shard_map/all_gather | solution.py:194
  160.3 1.3 copy-start.17
  177.3 195.9 %all-reduce.9.cloned.1.call-start = ((), (), s32[]{:S(2)}) async-start(), calls=%async_computation.13 | async-start | bytes 10485760
  243.0 3.0 copy-start.5
  243.0 3.0 copy-start.8
  249.0 145.5 %copy-start.4 = (bf16[128,1280]{1,0:T(8,128)(2,1)S(1)}, bf16[128,1280]{1,0:T(8,128)(2,1)}, u32[]{:S(2)}) copy-start(bf16[128,1280]{1,0:T(8,128)(2,1)} %copy-done.3) | copy-start | bytes 983044
  249.0 145.5 %copy-start.22 = (f32[128]{0:T(128)S(1)}, f32[128]{0:T(128)}, u32[]{:S(2)}) copy-start(f32[128]{0:T(128)} %copy-done.21) | copy-start | bytes 1540
  249.1 151.9 %copy-start.16 = (pred[64,128,2]{1,0,2:T(32,128)(4,1)S(1)}, pred[64,128,2]{1,0,2:T(32,128)(4,1)}, u32[]{:S(2)}) copy-start(pred[64,128,2]{1,0,2:T(32,128)(4,1)} %get-tuple-element.212) | copy-start | bytes 49156
  249.1 152.2 %copy-start.18 = (f32[128]{0:T(128)S(1)}, f32[128]{0:T(128)}, u32[]{:S(2)}) copy-start(f32[128]{0:T(128)} %copy-done.17) | copy-start | bytes 1540
  375.5 13.7 %all-to-all-start.3 = ((bf16[16,2,2,1280]{3,2,1,0:T(2,128)(2,1)}), bf16[16,2,2,1280]{3,2,1,0:T(2,128)(2,1)S(1)}, u32[]{:S(2)}, u32[]{:S(2)}) async-start(bf16[16,2,2,1280]{3,2,1,0:T(2,128)(2,1)} %copy.57), calls=%async_computation.4 | async-start | bytes 327680 | tf_op jit(solution)/shard_map/all_to_all | solution.py:106
  389.3 11.6 %all-to-all-start.1 = ((bf16[16,2,2,1280]{3,2,1,0:T(2,128)(2,1)}), bf16[16,2,2,1280]{3,2,1,0:T(2,128)(2,1)S(1)}, u32[]{:S(2)}, u32[]{:S(2)}) async-start(bf16[16,2,2,1280]{3,2,1,0:T(2,128)(2,1)} %copy.54), calls=%async_computation.2 | async-start | bytes 327680 | tf_op jit(solution)/shard_map/all_to_all | solution.py:106
  394.4 50.9 %all-gather.9.cloned.1.call-start = ((), (), s32[]{:S(2)}) async-start(), calls=%async_computation.8 | async-start | bytes 5570560 | tf_op jit(solution)/shard_map/all_gather | solution.py:213
  394.6 11.7 %copy-start.11 = (bf16[16,16,2,2,320]{4,1,3,0,2:T(8,128)(2,1)S(1)}, bf16[16,16,2,2,320]{4,1,3,0,2:T(8,128)(2,1)}, u32[]{:S(2)}) copy-start(bf16[16,16,2,2,320]{4,1,3,0,2:T(8,128)(2,1)} %copy-done.10) | copy-start | bytes 1966084
  404.3 137.2 %all-reduce.7.cloned.1.call-start = ((), (), s32[]{:S(2)}) async-start(), calls=%async_computation.12 | async-start | bytes 409600
  449.5 5.6 copy-start.12
  449.5 5.6 copy-start.14
  449.5 173.2 %reduce-scatter.14.cloned.1.call-start = ((), (), s32[]{:S(2)}) async-start(), calls=%async_computation.11 | async-start | bytes 696320
  455.1 1.0 copy-start.15
  461.0 1.0 copy-start.15
  466.9 1.0 copy-start.15
  478.9 5.1 copy-start.9
  484.0 4.1 copy-start.23
  484.0 4.1 copy-start.24
  484.0 140.4 %copy-start.1 = (bf16[2,1280,320]{1,2,0:T(8,128)(2,1)S(1)}, bf16[2,1280,320]{1,2,0:T(8,128)(2,1)}, u32[]{:S(2)}) copy-start(bf16[2,1280,320]{1,2,0:T(8,128)(2,1)} %param.20) | copy-start | bytes 4915204
  (10 other events, 8.4 us)
Sparse Core Ops, SparseCore 0:
  11.7 46.2 all-gather.6
  76.4 63.3 reduce-scatter.11
  159.6 36.8 all-gather.10
  198.8 38.9 all-gather.12
  249.2 123.9 all-reduce.8
  404.4 40.8 all-gather.8
  449.6 91.7 all-reduce.6
  545.4 77.3 reduce-scatter.13
where the time goes:
time: 633 us; the launch traced here: 631 us
  waiting for transfers between devices  463 us (73%)
  matrix products  78.8 us (12%)
  blocking collectives  25.4 us (4%)
  local copies, waits for them, and re-layouts  22.2 us (4%)
  between operations  15.2 us (2%)
  starting transfers between devices  13.1 us (2%)
  other arithmetic  13 us (2%)
    unnamed x11, waiting for transfers between devices  256 us
    reduce_scatter x1, waiting for transfers between devices, shards(): lax.psum_scatter(jnp.einsum('hsk,hkd->sd', context, proj_weight, preferre...  62.2 us
    all_gather x1, waiting for transfers between devices, shards(): full_norm = lax.all_gather(normed, 'tensor', axis=0, tiled=True)  46.4 us
    all_gather x1, waiting for transfers between devices, shards(): lax.all_gather(grad_landed[None], 'tensor', axis=0, tiled=True)  36.6 us
    all_gather x1, waiting for transfers between devices, shards(): full_grad = lax.all_gather(grad_mid, 'tensor', axis=0, tiled=True)  35.1 us
    all_gather x1, waiting for transfers between devices, shards(): arrived = lax.all_gather(landed[None], 'tensor', axis=0, tiled=True)  19 us
    all_to_all x1, blocking collectives, shards(): lax.all_to_all(outgoing, 'dp', split_axis=0, concat_axis=0, tiled=True)  13.8 us
  transfers between devices with their start and end apart: 10, of which 10 were waited for; matrix products, arithmetic and copies ran while one was open for 10% of the time, Pallas kernels for 0%

commit v1 on v0

--- a/solution.py
+++ b/solution.py
@@ -210,7 +210,10 @@
         "pr,pd->rd", dispatch_rows, grad_back, preferred_element_type=jnp.float32
     )
     grad_mid = (upstream + norm_back(normal_mid, factor_mid, grad_norm)).astype(jnp.bfloat16)
-    full_grad = lax.all_gather(grad_mid, "tensor", axis=0, tiled=True)
+    devices = lax.axis_size("tensor")
+    blocks = jnp.stack([grad_mid for _ in range(devices)])
+    blocks = lax.all_to_all(blocks, "tensor", split_axis=0, concat_axis=0)
+    full_grad = jnp.concatenate(blocks, axis=0)
     grad_context = jnp.einsum(
         "sd,hkd->hsk", full_grad, proj_weight, preferred_element_type=jnp.float32
     ).astype(jnp.bfloat16)

time: 633 us -> 718 us (1.13)
  waiting for transfers between devices: 463 us -> 544 us
    all_to_all x0 -> x1, waiting for transfers between devices: none -> 111 us  [shards(): blocks = lax.all_to_all(blocks, 'tensor', split_axis=0, concat_axis=0)]
    all_gather x1 -> x0, waiting for transfers between devices: 35.1 us -> none  [shards(): full_grad = lax.all_gather(grad_mid, 'tensor', axis=0, tiled=True)]
    unnamed x11 -> x10, waiting for transfers between devices: 256 us -> 258 us
  transfers between devices with their start and end apart: 10 -> 10, of which waited for: 10 -> 10; matrix products, arithmetic and copies ran while one was open for 10% -> 8% of each run, Pallas kernels for 0% -> 0%
where the time goes in v1:
time: 718 us; the launch traced here: 717 us
  waiting for transfers between devices  544 us (76%)
  matrix products  76.2 us (11%)
  blocking collectives  25.3 us (4%)
  local copies, waits for them, and re-layouts  24.3 us (3%)
  starting transfers between devices  18.8 us (3%)
  between operations  15.2 us (2%)
  other arithmetic  13 us (2%)
    unnamed x10, waiting for transfers between devices  258 us
    all_to_all x1, waiting for transfers between devices, shards(): blocks = lax.all_to_all(blocks, 'tensor', split_axis=0, concat_axis=0)  111 us
    reduce_scatter x1, waiting for transfers between devices, shards(): lax.psum_scatter(jnp.einsum('hsk,hkd->sd', context, proj_weight, preferre...  62.2 us
    all_gather x1, waiting for transfers between devices, shards(): full_norm = lax.all_gather(normed, 'tensor', axis=0, tiled=True)  46.4 us
    all_gather x1, waiting for transfers between devices, shards(): lax.all_gather(grad_landed[None], 'tensor', axis=0, tiled=True)  36.6 us
    all_gather x1, waiting for transfers between devices, shards(): arrived = lax.all_gather(landed[None], 'tensor', axis=0, tiled=True)  19 us
  transfers between devices with their start and end apart: 10, of which 10 were waited for; matrix products, arithmetic and copies ran while one was open for 8% of the time, Pallas kernels for 0%

profile of v1, /device:TPU:2, one launch (start us, length us, event | category | flops | bytes accessed | tf_op | source)
XLA Modules:
  0.0 716.7 jit_solution(8876604840972868410)
XLA Ops:
  9.7 1.9 fusion.87
  11.7 46.4 %all-gather.6.cloned.1.call-done = bf16[2048,1280]{1,0:T(8,128)(2,1)} async-done(((bf16[128,1280]{1,0:T(8,128)(2,1)}), bf16[2048,1280]{1,0:T(8,128)(2,1)}) %all-gather.6.cloned.1.call-update) | async-done | bytes 5242896 | tf_op jit(solution)/shard_map/all_gather | solution.py:133
  58.0 4.2 fusion.47
  63.9 8.0 %while.25 = (s32[]{:T(128)}, bf16[4,1,512,80]{2,3,1,0:T(8,128)(2,1)S(1)}, bf16[4,1,512,80]{3,2,1,0:T(8,128)(2,1)S(1)}, bf16[1,2048,80]{2,1,0:T(8,128)(2,1)S(1)}, bf16[1,2048,80]{2,1,0:T(8,128)(2,1)}, /*index=5*/s32[]{:T(128)}) while((s32[]{:T(128)}, bf16[4,1,512,80]{2,3,1,0:T(8,128)(2,1)S(1)}, bf16[4,1,512,80]{3,2,1,0:T(8,128)(2,1)S(1)}, ...), condition=%wide.region_4.5_spmd, body=%wide.region_2.4_spmd.sunk | while | flops 340827648 | bytes 10965105 | solution.py:57
  72.3 4.0 convolution_convert_fusion.1
  77.6 62.2 %reduce-scatter.12.cloned.1.call-done = bf16[128,1280]{1,0:T(8,128)(2,1)} async-done(((bf16[2048,1280]{1,0:T(8,128)(2,1)}), bf16[128,1280]{1,0:T(8,128)(2,1)}) %reduce-scatter.12.cloned.1.call-update) | async-done | bytes 327696 | tf_op jit(solution)/shard_map/reduce_scatter | solution.py:145
  141.7 1.7 convolution_convert_fusion.8
  145.1 13.7 %all_to_all.25 = bf16[16,2,2,1280]{3,2,1,0:T(2,128)(2,1)S(1)} all-to-all(bf16[16,2,2,1280]{3,2,1,0:T(2,128)(2,1)} %reshape.177), channel_id=1, replica_groups=mesh['dp'=16,'tensor'=16] {'dp'}, dimensions={0} | all-to-all | bytes 327680 | tf_op jit(solution)/shard_map/all_to_all | solution.py:166
  165.0 11.6 %all_to_all.26 = bf16[16,2,2,1280]{3,2,1,0:T(2,128)(2,1)S(1)} all-to-all(bf16[16,2,2,1280]{3,2,1,0:T(2,128)(2,1)} %reshape.179), channel_id=1, replica_groups=mesh['dp'=16,'tensor'=16] {'dp'}, dimensions={0} | all-to-all | bytes 327680 | tf_op jit(solution)/shard_map/all_to_all | solution.py:193
  177.5 19.0 %all-gather.8.cloned.1.call-done = bf16[256,2,2,1280]{3,0,2,1:T(8,128)(2,1)} async-done(((bf16[16,2,2,1280]{3,0,2,1:T(8,128)(2,1)}), bf16[256,2,2,1280]{3,0,2,1:T(8,128)(2,1)}) %all-gather.8.cloned.1.call-update) | async-done | bytes 2621456 | tf_op jit(solution)/shard_map/all_gather | solution.py:167
  196.5 4.7 fusion.62
  201.2 36.6 %all-gather.10.cloned.1.call-done = bf16[256,2,2,1280]{3,0,2,1:T(8,128)(2,1)} async-done(((bf16[16,2,2,1280]{3,0,2,1:T(8,128)(2,1)}), bf16[256,2,2,1280]{3,0,2,1:T(8,128)(2,1)}) %all-gather.10.cloned.1.call-update) | async-done | bytes 2621456 | tf_op jit(solution)/shard_map/all_gather | solution.py:194
  237.8 4.3 fusion.60
  243.0 3.0 fusion.38
  246.0 3.1 fusion.37
  250.4 122.9 %all-reduce.9.cloned.1.call-done = (bf16[16,16,2,2,1280]{4,1,3,0,2:T(8,128)(2,1)}, bf16[16,16,2,2,1280]{4,1,3,0,2:T(8,128)(2,1)}) async-done(((bf16[16,16,2,2,1280]{4,1,3,0,2:T(8,128)(2,1)}, bf16[16,16,2,2,1280]{4,1,3,0,2:T(8,128)(2,1)}), (bf16[16,16,2,2,1280]{4,1,3,0,2:T(8,128)(2,1)}, bf16[16,16,2,2,1280]{4,1,3,0,2:T(8,128)(2,1)})) %all-reduce.9.cloned.1.call-update) | async-done | bytes 5242896
  375.7 7.3 %all-to-all-start.3 = ((bf16[16,2,2,1280]{3,2,1,0:T(2,128)(2,1)}), bf16[16,2,2,1280]{3,2,1,0:T(2,128)(2,1)S(1)}, u32[]{:S(2)}, u32[]{:S(2)}) async-start(bf16[16,2,2,1280]{3,2,1,0:T(2,128)(2,1)} %copy.57), calls=%async_computation.4 | async-start | bytes 327680 | tf_op jit(solution)/shard_map/all_to_all | solution.py:106
  385.3 4.1 all-to-all-done.3
  389.4 5.1 all-to-all-start.1
  395.0 6.0 all-to-all-done.1
  401.4 1.7 fusion.90
  403.2 2.8 stack.11
  406.0 5.7 all-to-all-start.4
  413.0 4.0 fusion.40
  417.0 111.5 %all-to-all-done.4 = bf16[16,128,1280]{2,1,0:T(8,128)(2,1)} async-done(((bf16[16,128,1280]{2,1,0:T(8,128)(2,1)}), bf16[16,128,1280]{2,1,0:T(8,128)(2,1)}, u32[]{:S(2)}, u32[]{:S(2)}) %all-to-all-start.4) | async-done | bytes 5242912 | tf_op jit(solution)/shard_map/all_to_all | solution.py:215
  528.5 4.2 fusion.50
  532.7 4.3 fusion.49
  538.3 23.7 %while.26 = (s32[]{:T(128)}, f32[1,2048,80]{1,2,0:T(8,128)S(1)}, f32[1,2048,80]{1,2,0:T(8,128)S(1)}, bf16[4,1,512,80]{2,3,1,0:T(8,128)(2,1)S(1)}, bf16[4,1,512,8...) while((s32[]{:T(128)}, f32[1,2048,80]{1,2,0:T(8,128)S(1)}, ...), condition=%wide.region_17.18_spmd.clone, body=%wide.region_14.17_spmd.clone.sunk | while | flops 855284736 | bytes 37580964 | solution.py:92
  562.1 4.0 convolution_convert_fusion.4
  567.2 4.1 fusion.39
  571.9 55.1 %all-reduce.7.cloned.1.call-done = bf16[1,80,1280]{2,1,0:T(8,128)(2,1)} async-done(((bf16[1,80,1280]{2,1,0:T(8,128)(2,1)}), bf16[1,80,1280]{2,1,0:T(8,128)(2,1)}) %all-reduce.7.cloned.1.call-update) | async-done | bytes 204816
  628.5 79.8 %reduce-scatter.14.cloned.1.call-done = bf16[80,240]{1,0:T(8,128)(2,1)} async-done(((bf16[1280,240]{1,0:T(8,128)(2,1)}), bf16[80,240]{1,0:T(8,128)(2,1)}) %reduce-scatter.14.cloned.1.call-update) | async-done | bytes 38416
  (162 shorter events, 62.3 us)
Async XLA Ops:
  7.2 189.4 %copy-start = (bf16[2,1280,320]{1,2,0:T(8,128)(2,1)S(1)}, bf16[2,1280,320]{1,2,0:T(8,128)(2,1)}, u32[]{:S(2)}) copy-start(bf16[2,1280,320]{1,2,0:T(8,128)(2,1)} %param.20) | copy-start | bytes 4915204
  7.2 50.8 %all-gather.6.cloned.1.call-start = ((), (), s32[]{:S(2)}) async-start(), calls=%async_computation.7 | async-start | bytes 5570560 | tf_op jit(solution)/shard_map/all_gather | solution.py:133
  11.6 128.2 %reduce-scatter.12.cloned.1.call-start = ((), (), s32[]{:S(2)}) async-start(), calls=%async_computation.8 | async-start | bytes 5570560 | tf_op jit(solution)/shard_map/reduce_scatter | solution.py:145
  63.9 8.4 %copy-start.7 = (bf16[1,80,1280]{2,1,0:T(8,128)(2,1)S(1)}, bf16[1,80,1280]{2,1,0:T(8,128)(2,1)}, u32[]{:S(2)}) copy-start(bf16[1,80,1280]{2,1,0:T(8,128)(2,1)} %param.19) | copy-start | bytes 614404
  63.9 1.1 copy-start.13
  76.2 63.5 %copy-start.2 = (bf16[128,1280]{1,0:T(8,128)(2,1)S(1)}, bf16[128,1280]{1,0:T(8,128)(2,1)}, u32[]{:S(2)}) copy-start(bf16[128,1280]{1,0:T(8,128)(2,1)} %param.13) | copy-start | bytes 983044
  76.3 120.3 %all-gather.8.cloned.1.call-start = ((), (), s32[]{:S(2)}) async-start(), calls=%async_computation.9 | async-start | bytes 2785280 | tf_op jit(solution)/shard_map/all_gather | solution.py:167
  140.9 20.7 %copy-start.6 = (bf16[128,1280]{1,0:T(8,128)(2,1)S(1)}, bf16[128,1280]{1,0:T(8,128)(2,1)}, u32[]{:S(2)}) copy-start(bf16[128,1280]{1,0:T(8,128)(2,1)} %param.14) | copy-start | bytes 983044
  159.5 78.3 %all-gather.10.cloned.1.call-start = ((), (), s32[]{:S(2)}) async-start(), calls=%async_computation.10 | async-start | bytes 2785280 | tf_op jit(solution)/shard_map/all_gather | solution.py:194
  160.3 1.3 copy-start.18
  177.3 196.0 %all-reduce.9.cloned.1.call-start = ((), (), s32[]{:S(2)}) async-start(), calls=%async_computation.13 | async-start | bytes 10485760
  243.0 3.0 copy-start.5
  243.0 3.0 copy-start.8
  249.1 145.5 %copy-start.4 = (bf16[128,1280]{1,0:T(8,128)(2,1)S(1)}, bf16[128,1280]{1,0:T(8,128)(2,1)}, u32[]{:S(2)}) copy-start(bf16[128,1280]{1,0:T(8,128)(2,1)} %copy-done.3) | copy-start | bytes 983044
  249.1 145.5 %copy-start.17 = (bf16[64,128,2]{1,0,2:T(8,128)(2,1)S(1)}, bf16[64,128,2]{1,0,2:T(8,128)(2,1)}, u32[]{:S(2)}) copy-start(bf16[64,128,2]{1,0,2:T(8,128)(2,1)} %get-tuple-element.213) | copy-start | bytes 98308
  249.1 145.5 %copy-start.23 = (f32[128]{0:T(128)S(1)}, f32[128]{0:T(128)}, u32[]{:S(2)}) copy-start(f32[128]{0:T(128)} %copy-done.22) | copy-start | bytes 1540
  249.2 151.9 %copy-start.16 = (pred[64,128,2]{1,0,2:T(32,128)(4,1)S(1)}, pred[64,128,2]{1,0,2:T(32,128)(4,1)}, u32[]{:S(2)}) copy-start(pred[64,128,2]{1,0,2:T(32,128)(4,1)} %get-tuple-element.212) | copy-start | bytes 49156
  249.2 152.2 %copy-start.19 = (f32[128]{0:T(128)S(1)}, f32[128]{0:T(128)}, u32[]{:S(2)}) copy-start(f32[128]{0:T(128)} %copy-done.18) | copy-start | bytes 1540
  375.7 13.7 %all-to-all-start.3 = ((bf16[16,2,2,1280]{3,2,1,0:T(2,128)(2,1)}), bf16[16,2,2,1280]{3,2,1,0:T(2,128)(2,1)S(1)}, u32[]{:S(2)}, u32[]{:S(2)}) async-start(bf16[16,2,2,1280]{3,2,1,0:T(2,128)(2,1)} %copy.57), calls=%async_computation.4 | async-start | bytes 327680 | tf_op jit(solution)/shard_map/all_to_all | solution.py:106
  389.4 11.6 %all-to-all-start.1 = ((bf16[16,2,2,1280]{3,2,1,0:T(2,128)(2,1)}), bf16[16,2,2,1280]{3,2,1,0:T(2,128)(2,1)S(1)}, u32[]{:S(2)}, u32[]{:S(2)}) async-start(bf16[16,2,2,1280]{3,2,1,0:T(2,128)(2,1)} %copy.54), calls=%async_computation.2 | async-start | bytes 327680 | tf_op jit(solution)/shard_map/all_to_all | solution.py:106
  406.0 5.8 copy-start.26
  406.0 7.0 copy-start.11
  406.0 122.4 %all-to-all-start.4 = ((bf16[16,128,1280]{2,1,0:T(8,128)(2,1)}), bf16[16,128,1280]{2,1,0:T(8,128)(2,1)}, u32[]{:S(2)}, u32[]{:S(2)}) async-start(bf16[16,128,1280]{2,1,0:T(8,128)(2,1)} %stack.11), calls=%async_computation.5 | async-start | bytes 10485760 | tf_op jit(solution)/shard_map/all_to_all | solution.py:215
  411.7 215.3 %all-reduce.7.cloned.1.call-start = ((), (), s32[]{:S(2)}) async-start(), calls=%async_computation.12 | async-start | bytes 409600
  532.7 5.6 copy-start.12
  532.7 5.6 copy-start.14
  537.0 171.3 %reduce-scatter.14.cloned.1.call-start = ((), (), s32[]{:S(2)}) async-start(), calls=%async_computation.11 | async-start | bytes 696320
  544.2 1.0 copy-start.15
  562.1 5.1 copy-start.9
  567.2 4.1 copy-start.24
  567.2 4.1 copy-start.25
  567.2 142.7 %copy-start.1 = (bf16[2,1280,320]{1,2,0:T(8,128)(2,1)S(1)}, bf16[2,1280,320]{1,2,0:T(8,128)(2,1)}, u32[]{:S(2)}) copy-start(bf16[2,1280,320]{1,2,0:T(8,128)(2,1)} %param.20) | copy-start | bytes 4915204
  (12 other events, 10.4 us)
Sparse Core Ops, SparseCore 0:
  11.7 46.2 all-gather.5
  76.4 63.3 reduce-scatter.11
  159.6 36.8 all-gather.7
  198.8 38.9 all-gather.9
  249.3 123.9 all-reduce.8
  537.1 89.8 all-reduce.6
  630.9 77.3 reduce-scatter.13
